TPU v7x, 32 devices: a whole 2x2x4 slice. The times are simulated.
32 devices in a mesh: stem: 8 (over y, x, core), grp: 4 (over z).
Axes of the slice: x: 2, y: 2, z: 4, core: 2. Of those that a mesh axis runs over, the one named last changes fastest.
Arguments:
- stem_tensor: float32 [32, 512, 512], P(None, 'stem', 'grp'), may hold values from -6 to 6
- left_factors: float32 [2, 16, 16, 256], P(None, 'grp'), may hold values from -0.375 to 0.375
- right_factors: float32 [2, 256, 1024], replicated, may hold values from -0.1875 to 0.1875
- index_labels: int32 [2, 9], replicated, may hold values from 0 to 8, each once within a row
Outputs:
- contracted: float32 [32, 512, 512], P(('stem', 'grp'))
Inputs may be any that keep to these rules, and one draw needn't show every extreme that they name: `index_labels`: each row is a permutation of 0 to 8.
All inputs are finite; a program needn't handle non-finite values.
Results may differ from a plain program's by a relative error of at most 0.000098.
Values sent between devices are 32-bit elements; how exact they have to be, the bound alone decides.
No kernel may reach another device: no remote copies, remote signals or barrier semaphores. Data moves between devices by JAX's collectives and lax.ppermute only.
A program may use at most 64 MiB of HBM per device.

v0:
```python
import jax
import jax.numpy as jnp
from jax import lax
from jax.sharding import PartitionSpec as P

LOW = 32


def assemble(left, right):
    upper = left.shape[1]
    table = right.reshape(right.shape[0], LOW, LOW)
    product = jnp.einsum("abk,kcd->acbd", left, table, precision=lax.Precision.HIGHEST)
    return product.reshape(left.shape[0] * LOW, upper * LOW)


def relabel(branch, bit_order):
    row_ids = jnp.arange(branch.shape[0], dtype=jnp.int32)
    source_rows = jnp.zeros_like(row_ids)
    for bit_number in range(bit_order.shape[0]):
        picked = jnp.bitwise_and(jnp.right_shift(row_ids, bit_number), 1)
        source_rows = source_rows + jnp.left_shift(picked, bit_order[bit_number])
    return jnp.take(branch, source_rows, axis=0)


def contract_last(tensor, branch):
    dims = tensor.shape
    flat = jnp.dot(tensor.reshape(-1, dims[-1]), branch, precision=lax.Precision.HIGHEST)
    return flat.reshape(dims[:-1] + (branch.shape[1],))


def on_device(stem_tensor, left_factors, right_factors, index_labels):
    whole_left = lax.all_gather(left_factors, "grp", axis=1, tiled=True)
    branches = jnp.stack(
        [assemble(whole_left[branch_id], right_factors[branch_id]) for branch_id in range(2)]
    )
    branch_one = relabel(branches[0], index_labels[0])
    branch_two = relabel(branches[1], index_labels[1])
    stem_count = lax.axis_size("stem")
    open_rows, outer_local, inner_local = stem_tensor.shape
    shaped = stem_tensor.reshape(stem_count, open_rows // stem_count, outer_local, inner_local)
    regrouped = lax.all_to_all(shaped, "grp", split_axis=1, concat_axis=3, tiled=True)
    halfway = contract_last(regrouped, branch_one)
    gathered_modes = lax.all_to_all(halfway, "stem", split_axis=0, concat_axis=2, tiled=True)
    slab = gathered_modes[0]
    return lax.dot_general(
        slab, branch_two, (((1,), (0,)), ((), ())), precision=lax.Precision.HIGHEST
    )


def solution(mesh):
    placed = (P(None, "stem", "grp"), P(None, "grp", None, None), P(), P())
    return jax.shard_map(
        on_device,
        mesh=mesh,
        in_specs=placed,
        out_specs=P(("stem", "grp"), None, None),
        check_vma=False,
    )
```

profile of v0, /device:TPU:0, one launch (start us, length us, event | category | flops | bytes accessed | tf_op | source)
XLA Modules:
  0.0 91.7 jit_solution(12908365413325150748)
XLA Ops:
  0.0 2.3 %copy.20 = f32[8,4,64,128]{3,2,0,1:T(8,128)} copy(f32[8,4,64,128]{3,2,1,0:T(8,128)} %bitcast.70) | data formatting | bytes 2097152 | tf_op jit(solution)/shard_map/reshape | solution.py:40
  2.3 0.0 copy-start.2
  2.3 6.5 %all-to-all-start = ((f32[8,4,64,128]{3,2,0,1:T(8,128)}), f32[8,4,64,128]{3,2,0,1:T(8,128)S(1)}, u32[]{:S(2)}, u32[]{:S(2)}) async-start(f32[8,4,64,128]{3,2,0,1:T(8,128)} %copy.20), calls=%async_computation | async-start | bytes 2097152 | tf_op jit(solution)/shard_map/all_to_all | solution.py:41
  8.8 2.7 %fusion.11 = (f32[1,256,1024]{2,1,0:T(8,128)}, f32[1,256,1024]{2,1,0:T(8,128)S(1)}) fusion(f32[2,256,1024]{2,1,0:T(8,128)} %param.8), kind=kLoop, calls=%fused_computation.33 | loop fusion | bytes 4194304 | tf_op jit(solution)/shard_map/slice | solution.py:34
  11.5 0.3 copy.18
  11.8 0.0 copy-done.2
  11.8 33.1 %all_gather.3 = f32[2,16,16,256]{3,2,1,0:T(8,128)S(1)} all-gather(f32[2,4,16,256]{3,2,1,0:T(8,128)S(1)} %copy-done.2), channel_id=1, replica_groups=mesh['stem'=8,'grp'=4] {'grp'}, dimensions={1}, use_global_device_ids=true | all-gather | bytes 655360 | tf_op jit(solution)/shard_map/all_gather | solution.py:32
  44.9 0.0 copy-start.1
  44.9 0.8 copy-done.1
  45.7 3.4 %convolution_bitcast_fusion.1 = f32[16,32,16,32]{3,2,0,1:T(8,128)S(1)} fusion(f32[256,32,32,1]{0,2,3,1:T(8,128)S(1)} %bitcast.68, f32[2,16,16,256]{3,2,1,0:T(8,128)S(1)} %all_gather.3), kind=kOutput, calls=%fused_computation.3 | convolution fusion | flops 805306368 | bytes 2359296 | tf_op jit(solution)/shard_map/abk,kcd->acbd/dot_general | solution.py:12
  49.2 2.4 %copy.19 = f32[16,32,16,32]{3,2,1,0:T(8,128)} copy(f32[16,32,16,32]{3,2,0,1:T(8,128)S(1)} %convolution_bitcast_fusion.1) | data formatting | bytes 2097152 | tf_op jit(solution)/shard_map/abk,kcd->acbd/transpose | solution.py:12
  51.6 0.0 copy-start.3
  51.6 3.6 %squeeze_stack_reshape.6 = f32[512,512]{1,0:T(8,128)S(1)} reshape(f32[16,32,16,32]{3,2,1,0:T(8,128)} %copy.19) | data formatting | bytes 2097152 | tf_op jit(solution)/shard_map/squeeze;stack;reshape | solution.py:36
  55.1 0.0 copy-done.3
  55.2 0.7 fusion.12
  55.9 5.6 %compare_and_fusion.1 = (pred[512]{0:T(512)(128)(4,1)S(1)}, s32[512]{0:T(512)S(1)}) fusion(s32[]{:T(128)} %bitcast.8, s32[]{:T(128)} %bitcast.7, s32[]{:T(128)} %bitcast.6, s32[]{:T(128)} %bitcast.5, s32[]{:T(128)} %bitcast.4, s32[]{:T(128)} %bitcast.3, s32[]{:T(128)} %bitcast.2, s32[]{:T(128)} %bitcast.1, s32[]{:T(128)} %bitcast), kind=kLoop, calls=%fused_computation.30 | loop fusion | flops 20992 | bytes 2596 | tf_op jit(solution)/shard_map/jit(_take)/and | solution.py:22
  61.5 1.6 %gather_fusion = f32[512,512]{1,0:T(8,128)S(1)} fusion(f32[512,512]{1,0:T(8,128)S(1)} %squeeze_stack_reshape.6, s32[1024]{0:T(1024)S(1)} %pad_clamp_fusion.1), kind=kCustom, calls=%fused_computation.clone | custom fusion | bytes 2099200 | tf_op jit(solution)/shard_map/jit(_take)/gather | solution.py:22
  63.2 0.0 copy-start
  63.2 0.0 all-to-all-done
  63.2 0.7 copy.21
  63.9 3.0 %fusion = f32[512,512]{0,1:T(8,128)} fusion(f32[64,8,4,128]{3,2,1,0:T(4,128)S(1)} %bitcast.67, f32[512,512]{1,0:T(8,128)S(1)} %gather_fusion, pred[512]{0:T(512)(128)(4,1)S(1)} %get-tuple-element.8), kind=kOutput, calls=%fused_computation.5 | convolution fusion | flops 1610874880 | bytes 3146240 | tf_op jit(solution)/shard_map/dot_general | solution.py:27
  66.9 3.7 %all-to-all-start.1 = ((f32[8,1,64,512]{3,2,1,0:T(8,128)}), f32[8,1,64,512]{3,2,1,0:T(8,128)S(1)}, u32[]{:S(2)}, u32[]{:S(2)}) async-start(f32[8,1,64,512]{3,2,1,0:T(8,128)} %bitcast.20), calls=%async_computation.1 | async-start | bytes 2097152 | tf_op jit(solution)/shard_map/all_to_all | solution.py:43
  70.6 0.0 copy-done
  70.6 0.3 copy.23
  71.0 4.4 %convolution_bitcast_fusion = f32[16,32,16,32]{3,2,0,1:T(8,128)S(1)} fusion(f32[256,32,32,1]{0,2,3,1:T(8,128)S(1)} %bitcast.69, f32[2,16,16,256]{3,2,1,0:T(8,128)} %copy-done.1), kind=kOutput, calls=%fused_computation.2 | convolution fusion | flops 805306368 | bytes 2359296 | tf_op jit(solution)/shard_map/abk,kcd->acbd/dot_general | solution.py:12
  75.4 2.4 %copy.24 = f32[16,32,16,32]{3,2,1,0:T(8,128)} copy(f32[16,32,16,32]{3,2,0,1:T(8,128)S(1)} %convolution_bitcast_fusion) | data formatting | bytes 2097152 | tf_op jit(solution)/shard_map/abk,kcd->acbd/transpose | solution.py:12
  77.8 3.5 %squeeze_stack_reshape.7 = f32[512,512]{1,0:T(8,128)S(1)} reshape(f32[16,32,16,32]{3,2,1,0:T(8,128)} %copy.24) | data formatting | bytes 2097152 | tf_op jit(solution)/shard_map/squeeze;stack;reshape | solution.py:37
  81.3 5.6 %compare_and_fusion = (pred[512]{0:T(512)(128)(4,1)S(1)}, s32[512]{0:T(512)S(1)}) fusion(s32[]{:T(128)} %bitcast.30, s32[]{:T(128)} %bitcast.29, s32[]{:T(128)} %bitcast.28, s32[]{:T(128)} %bitcast.27, s32[]{:T(128)} %bitcast.26, s32[]{:T(128)} %bitcast.25, s32[]{:T(128)} %bitcast.24, s32[]{:T(128)} %bitcast.23, s32[]{:T(128)} %bitcast.22), kind=kLoop, calls=%fused_computation.29 | loop fusion | flops 20992 | bytes 2596 | tf_op jit(solution)/shard_map/jit(_take)/and | solution.py:22
  87.0 1.6 %gather_fusion.1 = f32[512,512]{1,0:T(8,128)S(1)} fusion(f32[512,512]{1,0:T(8,128)S(1)} %squeeze_stack_reshape.7, s32[1024]{0:T(1024)S(1)} %pad_clamp_fusion), kind=kCustom, calls=%fused_computation.1.clone | custom fusion | bytes 2099200 | tf_op jit(solution)/shard_map/jit(_take)/gather | solution.py:22
  88.6 0.0 all-to-all-done.1
  88.6 3.1 %convolution_bitcast_fusion.2 = f32[1,512,512]{2,1,0:T(8,128)} fusion(f32[512,512]{1,0:T(8,128)S(1)} %bitcast.66, f32[512,512]{1,0:T(8,128)S(1)} %gather_fusion.1, pred[512]{0:T(512)(128)(4,1)S(1)} %get-tuple-element.6), kind=kOutput, calls=%fused_computation.4 | convolution fusion | flops 1610874880 | bytes 3146240 | tf_op jit(solution)/shard_map/dot_general | solution.py:45
  (2 shorter events, 0.0 us)
Async XLA Ops:
  2.3 9.5 %copy-start.2 = (f32[2,4,16,256]{3,2,1,0:T(8,128)S(1)}, f32[2,4,16,256]{3,2,1,0:T(8,128)}, u32[]{:S(2)}) copy-start(f32[2,4,16,256]{3,2,1,0:T(8,128)} %param.7) | copy-start | bytes 393220
  2.3 60.9 %all-to-all-start = ((f32[8,4,64,128]{3,2,0,1:T(8,128)}), f32[8,4,64,128]{3,2,0,1:T(8,128)S(1)}, u32[]{:S(2)}, u32[]{:S(2)}) async-start(f32[8,4,64,128]{3,2,0,1:T(8,128)} %copy.20), calls=%async_computation | async-start | bytes 2097152 | tf_op jit(solution)/shard_map/all_to_all | solution.py:41
  44.9 0.8 copy-start.1
  51.6 3.6 %copy-start.3 = (s32[2,9]{1,0:T(2,128)S(1)}, s32[2,9]{1,0:T(2,128)}, u32[]{:S(2)}) copy-start(s32[2,9]{1,0:T(2,128)} %param.9) | copy-start | bytes 220
  63.2 7.5 %copy-start = (f32[1,256,1024]{2,1,0:T(8,128)S(1)}, f32[1,256,1024]{2,1,0:T(8,128)}, u32[]{:S(2)}) copy-start(f32[1,256,1024]{2,1,0:T(8,128)} %get-tuple-element.10) | copy-start | bytes 3145732
  66.9 21.7 %all-to-all-start.1 = ((f32[8,1,64,512]{3,2,1,0:T(8,128)}), f32[8,1,64,512]{3,2,1,0:T(8,128)S(1)}, u32[]{:S(2)}, u32[]{:S(2)}) async-start(f32[8,1,64,512]{3,2,1,0:T(8,128)} %bitcast.20), calls=%async_computation.1 | async-start | bytes 2097152 | tf_op jit(solution)/shard_map/all_to_all | solution.py:43
where the time goes:
time: 92.3 us; the launch traced here: 91.7 us
  blocking collectives  33.1 us (36%)
  local copies, waits for them, and re-layouts  23.1 us (25%)
  matrix products  13.9 us (15%)
  other arithmetic  11.3 us (12%)
  starting transfers between devices  10.2 us (11%)
    all_gather x1, blocking collectives, on_device(): whole_left = lax.all_gather(left_factors, 'grp', axis=1, tiled=True)  33.1 us
    and x2, other arithmetic, relabel(): return jnp.take(branch, source_rows, axis=0)  11.3 us
    dot_general x2, matrix products, assemble(): jnp.einsum('abk,kcd->acbd', left, table, precision=lax.Precision.HIGHEST)  7.84 us
    all_to_all x1, starting transfers between devices, on_device(): lax.all_to_all(shaped, 'grp', split_axis=1, concat_axis=3, tiled=True)  6.48 us
    transpose x2, local copies, waits for them, and re-layouts, assemble(): jnp.einsum('abk,kcd->acbd', left, table, precision=lax.Precision.HIGHEST)  4.82 us
    all_to_all x1, starting transfers between devices, on_device(): lax.all_to_all(halfway, 'stem', split_axis=0, concat_axis=2, tiled=True)  3.74 us
    another operation x1, local copies, waits for them, and re-layouts, on_device(): branch_one = relabel(branches[0], index_labels[0])  3.56 us
    another operation x1, local copies, waits for them, and re-layouts, on_device(): branch_two = relabel(branches[1], index_labels[1])  3.54 us
  transfers between devices with their start and end apart: 2, of which 0 were waited for; matrix products, arithmetic and copies ran while one was open for 42% of the time, Pallas kernels for 0%

commit v1 on v0

--- a/solution.py
+++ b/solution.py
@@ -29,7 +29,12 @@
 
 
 def on_device(stem_tensor, left_factors, right_factors, index_labels):
-    whole_left = lax.all_gather(left_factors, "grp", axis=1, tiled=True)
+    ring = [left_factors]
+    for hop in range(3):
+        ring.append(lax.ppermute(ring[-1], "grp", [(dev, (dev + 1) % 4) for dev in range(4)]))
+    whole_left = jnp.roll(
+        jnp.concatenate(ring[::-1], axis=1), (lax.axis_index("grp") + 1) * ring[0].shape[1], axis=1
+    )
     branches = jnp.stack(
         [assemble(whole_left[branch_id], right_factors[branch_id]) for branch_id in range(2)]
     )

time: 92.3 us -> 85.1 us (0.922)
  blocking collectives: 33.1 us -> 0 us
  waiting for transfers between devices: 0.01 us -> 18.2 us
  starting transfers between devices: 10.2 us -> 16 us
  matrix products: 13.9 us -> 18.3 us
  local copies, waits for them, and re-layouts: 23.1 us -> 20.3 us
    all_gather x1 -> x0, blocking collectives: 33.1 us -> none  [on_device(): whole_left = lax.all_gather(left_factors, 'grp', axis=1, tiled=True)]
    ppermute x0 -> x3, waiting for transfers between devices: none -> 18.2 us  [on_device(): lax.ppermute(ring[-1], 'grp', [(dev, (dev + 1) % 4) for dev in range(4)])]
    ppermute x0 -> x3, starting transfers between devices: none -> 8.3 us  [on_device(): lax.ppermute(ring[-1], 'grp', [(dev, (dev + 1) % 4) for dev in range(4)])]
    transpose x2 -> x0, local copies, waits for them, and re-layouts: 4.82 us -> none  [assemble(): jnp.einsum('abk,kcd->acbd', left, table, precision=lax.Precision.HIGHEST)]
    dot_general x2, matrix products: 7.84 us -> 12.3 us  [assemble(): jnp.einsum('abk,kcd->acbd', left, table, precision=lax.Precision.HIGHEST)]
    all_to_all x1, starting transfers between devices: 6.48 us -> 3.99 us  [on_device(): lax.all_to_all(shaped, 'grp', split_axis=1, concat_axis=3, tiled=True)]
    unnamed x8 -> x15, local copies, waits for them, and re-layouts: 0.84 us -> 2.9 us
  transfers between devices with their start and end apart: 2 -> 5, of which waited for: 0 -> 1; matrix products, arithmetic and copies ran while one was open for 42% -> 50% of each run, Pallas kernels for 0% -> 0%
where the time goes in v1:
time: 85.1 us; the launch traced here: 84.3 us
  local copies, waits for them, and re-layouts  20.3 us (24%)
  matrix products  18.3 us (22%)
  waiting for transfers between devices  18.2 us (21%)
  starting transfers between devices  16 us (19%)
  other arithmetic  11.1 us (13%)
    ppermute x3, waiting for transfers between devices, on_device(): lax.ppermute(ring[-1], 'grp', [(dev, (dev + 1) % 4) for dev in range(4)])  18.2 us
    dot_general x2, matrix products, assemble(): jnp.einsum('abk,kcd->acbd', left, table, precision=lax.Precision.HIGHEST)  12.3 us
    and x2, other arithmetic, relabel(): return jnp.take(branch, source_rows, axis=0)  11.1 us
    ppermute x3, starting transfers between devices, on_device(): lax.ppermute(ring[-1], 'grp', [(dev, (dev + 1) % 4) for dev in range(4)])  8.3 us
    all_to_all x1, starting transfers between devices, on_device(): lax.all_to_all(shaped, 'grp', split_axis=1, concat_axis=3, tiled=True)  3.99 us
    all_to_all x1, starting transfers between devices, on_device(): lax.all_to_all(halfway, 'stem', split_axis=0, concat_axis=2, tiled=True)  3.74 us
    another operation x1, local copies, waits for them, and re-layouts, on_device(): branch_two = relabel(branches[1], index_labels[1])  3.54 us
    another operation x1, local copies, waits for them, and re-layouts, on_device(): branch_one = relabel(branches[0], index_labels[0])  3.54 us
  transfers between devices with their start and end apart: 5, of which 1 were waited for; matrix products, arithmetic and copies ran while one was open for 50% of the time, Pallas kernels for 0%

profile of v1, /device:TPU:0, one launch (start us, length us, event | category | flops | bytes accessed | tf_op | source)
XLA Modules:
  0.0 84.3 jit_solution(15639400047145776291)
XLA Ops:
  0.0 3.1 %collective-permute-start = (f32[2,4,16,256]{3,2,1,0:T(8,128)}, f32[2,4,16,256]{3,2,1,0:T(8,128)S(1)}, u32[]{:S(2)}, u32[]{:S(2)}) collective-permute-start(f32[2,4,16,256]{3,2,1,0:T(8,128)} %param.7), channel_id=1, source_target_pairs={{0,1},{1,2},{2,3},{3,0},{4,5},{5,6},{6,7},{7,4},{8,9},{9,10},{10,1... | collective-permute-start | bytes 393224 | tf_op jit(solution)/shard_map/ppermute | solution.py:34
  3.1 0.0 copy-start.3
  3.1 2.3 %copy.15 = f32[8,4,64,128]{3,2,0,1:T(8,128)} copy(f32[8,4,64,128]{3,2,1,0:T(8,128)} %bitcast.70) | data formatting | bytes 2097152 | tf_op jit(solution)/shard_map/reshape | solution.py:45
  5.4 0.0 copy-start.1
  5.4 4.0 %all-to-all-start = ((f32[8,4,64,128]{3,2,0,1:T(8,128)}), f32[8,4,64,128]{3,2,0,1:T(8,128)S(1)}, u32[]{:S(2)}, u32[]{:S(2)}) async-start(f32[8,4,64,128]{3,2,0,1:T(8,128)} %copy.15), calls=%async_computation | async-start | bytes 2097152 | tf_op jit(solution)/shard_map/all_to_all | solution.py:46
  9.4 0.0 collective-permute-done
  9.4 2.0 %collective-permute-start.1 = (f32[2,4,16,256]{3,2,1,0:T(8,128)S(1)}, f32[2,4,16,256]{3,2,1,0:T(8,128)S(1)}, u32[]{:S(2)}, u32[]{:S(2)}) collective-permute-start(f32[2,4,16,256]{3,2,1,0:T(8,128)S(1)} %collective-permute-done), channel_id=1, source_target_pairs={{0,1},{1,2},{2,3},{3,0},{4,5},{5,6},{6,7},{7,4},{8,9},{9,10},{10,1... | collective-permute-start | bytes 393224 | tf_op jit(solution)/shard_map/ppermute | solution.py:34
  11.4 2.7 %fusion.13 = (f32[1,256,1024]{2,1,0:T(8,128)}, f32[1,256,1024]{2,1,0:T(8,128)S(1)}) fusion(f32[2,256,1024]{2,1,0:T(8,128)} %param.8), kind=kLoop, calls=%fused_computation.43 | loop fusion | bytes 4194304 | tf_op jit(solution)/shard_map/slice | solution.py:39
  14.1 0.0 copy-done.3
  14.1 0.7 fusion.14
  14.8 18.2 %collective-permute-done.1 = f32[2,4,16,256]{3,2,1,0:T(8,128)S(1)} collective-permute-done((f32[2,4,16,256]{3,2,1,0:T(8,128)S(1)}, f32[2,4,16,256]{3,2,1,0:T(8,128)S(1)}, u32[]{:S(2)}, u32[]{:S(2)}) %collective-permute-start.1) | collective-permute-done | bytes 131104 | tf_op jit(solution)/shard_map/ppermute | solution.py:34
  33.0 3.2 %collective-permute-start.2 = (f32[2,4,16,256]{3,2,1,0:T(8,128)S(1)}, f32[2,4,16,256]{3,2,1,0:T(8,128)}, u32[]{:S(2)}, u32[]{:S(2)}) collective-permute-start(f32[2,4,16,256]{3,2,1,0:T(8,128)S(1)} %collective-permute-done.1), channel_id=1, source_target_pairs={{0,1},{1,2},{2,3},{3,0},{4,5},{5,6},{6,7},{7,4},{8,9},{9,10},{10,1... | collective-permute-start | bytes 393224 | tf_op jit(solution)/shard_map/ppermute | solution.py:34
  36.3 5.6 %compare_and_fusion.1 = (pred[512]{0:T(512)(128)(4,1)S(1)}, s32[512]{0:T(512)S(1)}) fusion(s32[]{:T(128)} %bitcast.8, s32[]{:T(128)} %bitcast.7, s32[]{:T(128)} %bitcast.6, s32[]{:T(128)} %bitcast.5, s32[]{:T(128)} %bitcast.4, s32[]{:T(128)} %bitcast.3, s32[]{:T(128)} %bitcast.2, s32[]{:T(128)} %bitcast.1, s32[]{:T(128)} %bitcast), kind=kLoop, calls=%fused_computation.38 | loop fusion | flops 20992 | bytes 2596 | tf_op jit(solution)/shard_map/jit(_take)/and | solution.py:22
  41.9 0.3 copy.14
  42.2 0.0 collective-permute-done.2
  42.2 0.9 %constant_dynamic-update-slice_fusion.7 = f32[2,32,16,256]{3,2,1,0:T(8,128)S(1)} fusion(f32[2,4,16,256]{3,2,1,0:T(8,128)} %collective-permute-done.2), kind=kLoop, calls=%fused_computation.23 | loop fusion | bytes 262144
  43.2 0.0 copy-done.1
  43.2 0.9 %constant_dynamic-update-slice_fusion.3 = f32[2,32,16,256]{3,2,1,0:T(8,128)S(1)} fusion(f32[2,32,16,256]{3,2,1,0:T(8,128)S(1)} %constant_dynamic-update-slice_fusion.4, f32[2,4,16,256]{3,2,1,0:T(8,128)} %collective-permute-done.2), kind=kLoop, calls=%fused_computation.19 | loop fusion | bytes 262144
  44.2 0.0 copy-start.2
  44.2 1.0 %copy-done.2 = f32[2,32,16,256]{3,2,1,0:T(8,128)} copy-done((f32[2,32,16,256]{3,2,1,0:T(8,128)}, f32[2,32,16,256]{3,2,1,0:T(8,128)S(1)}, u32[]{:S(2)}) %copy-start.2) | copy-done | bytes 1048600
  45.2 5.0 %convolution_bitcast_fusion.1 = f32[16,32,16,32]{3,2,1,0:T(8,128)} fusion(f32[256,32,32,1]{0,2,1,3:T(8,128)S(1)} %bitcast.68, f32[2,32,16,256]{3,2,1,0:T(8,128)S(1)} %constant_dynamic-update-slice_fusion, s32[]{:T(128)S(6)} %select_n.21), kind=kOutput, calls=%fused_computation.3 | convolution fusion | flops 805306368 | bytes 2359300 | tf_op jit(solution)/shard_map/abk,kcd->acbd/dot_general | solution.py:12
  50.2 3.5 %squeeze_stack_reshape.6 = f32[512,512]{1,0:T(8,128)S(1)} reshape(f32[16,32,16,32]{3,2,1,0:T(8,128)} %convolution_bitcast_fusion.1) | data formatting | bytes 2097152 | tf_op jit(solution)/shard_map/squeeze;stack;reshape | solution.py:41
  53.8 1.6 %gather_fusion = f32[512,512]{1,0:T(8,128)S(1)} fusion(f32[512,512]{1,0:T(8,128)S(1)} %squeeze_stack_reshape.6, s32[1024]{0:T(1024)S(1)} %pad_clamp_fusion.1), kind=kCustom, calls=%fused_computation.clone | custom fusion | bytes 2099200 | tf_op jit(solution)/shard_map/jit(_take)/gather | solution.py:22
  55.4 0.0 copy-start
  55.4 0.0 all-to-all-done
  55.4 0.7 copy.16
  56.1 3.0 %fusion = f32[512,512]{0,1:T(8,128)} fusion(f32[64,8,4,128]{3,2,1,0:T(4,128)S(1)} %bitcast.67, f32[512,512]{1,0:T(8,128)S(1)} %gather_fusion, pred[512]{0:T(512)(128)(4,1)S(1)} %get-tuple-element.8), kind=kOutput, calls=%fused_computation.5 | convolution fusion | flops 1610874880 | bytes 3146240 | tf_op jit(solution)/shard_map/dot_general | solution.py:27
  59.1 3.7 %all-to-all-start.1 = ((f32[8,1,64,512]{3,2,1,0:T(8,128)}), f32[8,1,64,512]{3,2,1,0:T(8,128)S(1)}, u32[]{:S(2)}, u32[]{:S(2)}) async-start(f32[8,1,64,512]{3,2,1,0:T(8,128)} %bitcast.20), calls=%async_computation.1 | async-start | bytes 2097152 | tf_op jit(solution)/shard_map/all_to_all | solution.py:48
  62.8 0.0 copy-done
  62.9 0.3 copy.18
  63.2 5.5 %compare_and_fusion = (pred[512]{0:T(512)(128)(4,1)S(1)}, s32[512]{0:T(512)S(1)}) fusion(s32[]{:T(128)} %bitcast.30, s32[]{:T(128)} %bitcast.29, s32[]{:T(128)} %bitcast.28, s32[]{:T(128)} %bitcast.27, s32[]{:T(128)} %bitcast.26, s32[]{:T(128)} %bitcast.25, s32[]{:T(128)} %bitcast.24, s32[]{:T(128)} %bitcast.23, s32[]{:T(128)} %bitcast.22), kind=kLoop, calls=%fused_computation.37 | loop fusion | flops 20992 | bytes 2596 | tf_op jit(solution)/shard_map/jit(_take)/and | solution.py:22
  68.7 7.3 %convolution_bitcast_fusion = f32[16,32,16,32]{3,2,1,0:T(8,128)} fusion(f32[256,32,32,1]{0,2,1,3:T(8,128)S(1)} %bitcast.69, f32[2,32,16,256]{3,2,1,0:T(8,128)} %copy-done.2, s32[]{:T(128)S(6)} %add.92, s32[]{:T(128)S(6)} %select_n.21), kind=kOutput, calls=%fused_computation.2 | convolution fusion | flops 805306368 | bytes 2359304 | tf_op jit(solution)/shard_map/abk,kcd->acbd/dot_general | solution.py:12
  76.0 3.5 %squeeze_stack_reshape.7 = f32[512,512]{1,0:T(8,128)S(1)} reshape(f32[16,32,16,32]{3,2,1,0:T(8,128)} %convolution_bitcast_fusion) | data formatting | bytes 2097152 | tf_op jit(solution)/shard_map/squeeze;stack;reshape | solution.py:42
  79.6 1.6 %gather_fusion.1 = f32[512,512]{1,0:T(8,128)S(1)} fusion(f32[512,512]{1,0:T(8,128)S(1)} %squeeze_stack_reshape.7, s32[1024]{0:T(1024)S(1)} %pad_clamp_fusion), kind=kCustom, calls=%fused_computation.1.clone | custom fusion | bytes 2099200 | tf_op jit(solution)/shard_map/jit(_take)/gather | solution.py:22
  81.2 0.0 all-to-all-done.1
  81.2 3.1 %convolution_bitcast_fusion.2 = f32[1,512,512]{2,1,0:T(8,128)} fusion(f32[512,512]{1,0:T(8,128)S(1)} %bitcast.66, f32[512,512]{1,0:T(8,128)S(1)} %gather_fusion.1, pred[512]{0:T(512)(128)(4,1)S(1)} %get-tuple-element.6), kind=kOutput, calls=%fused_computation.4 | convolution fusion | flops 1610874880 | bytes 3146240 | tf_op jit(solution)/shard_map/dot_general | solution.py:50
  (8 shorter events, 0.1 us)
Async XLA Ops:
  0.0 9.4 %collective-permute-start = (f32[2,4,16,256]{3,2,1,0:T(8,128)}, f32[2,4,16,256]{3,2,1,0:T(8,128)S(1)}, u32[]{:S(2)}, u32[]{:S(2)}) collective-permute-start(f32[2,4,16,256]{3,2,1,0:T(8,128)} %param.7), channel_id=1, source_target_pairs={{0,1},{1,2},{2,3},{3,0},{4,5},{5,6},{6,7},{7,4},{8,9},{9,10},{10,1... | collective-permute-start | bytes 393224 | tf_op jit(solution)/shard_map/ppermute | solution.py:34
  3.1 11.0 %copy-start.3 = (s32[2,9]{1,0:T(2,128)S(1)}, s32[2,9]{1,0:T(2,128)}, u32[]{:S(2)}) copy-start(s32[2,9]{1,0:T(2,128)} %param.9) | copy-start | bytes 220
  5.4 37.8 %copy-start.1 = (f32[2,4,16,256]{3,2,1,0:T(8,128)S(1)}, f32[2,4,16,256]{3,2,1,0:T(8,128)}, u32[]{:S(2)}) copy-start(f32[2,4,16,256]{3,2,1,0:T(8,128)} %param.7) | copy-start | bytes 393220
  5.4 50.0 %all-to-all-start = ((f32[8,4,64,128]{3,2,0,1:T(8,128)}), f32[8,4,64,128]{3,2,0,1:T(8,128)S(1)}, u32[]{:S(2)}, u32[]{:S(2)}) async-start(f32[8,4,64,128]{3,2,0,1:T(8,128)} %copy.15), calls=%async_computation | async-start | bytes 2097152 | tf_op jit(solution)/shard_map/all_to_all | solution.py:46
  9.4 23.7 %collective-permute-start.1 = (f32[2,4,16,256]{3,2,1,0:T(8,128)S(1)}, f32[2,4,16,256]{3,2,1,0:T(8,128)S(1)}, u32[]{:S(2)}, u32[]{:S(2)}) collective-permute-start(f32[2,4,16,256]{3,2,1,0:T(8,128)S(1)} %collective-permute-done), channel_id=1, source_target_pairs={{0,1},{1,2},{2,3},{3,0},{4,5},{5,6},{6,7},{7,4},{8,9},{9,10},{10,1... | collective-permute-start | bytes 393224 | tf_op jit(solution)/shard_map/ppermute | solution.py:34
  33.0 9.2 %collective-permute-start.2 = (f32[2,4,16,256]{3,2,1,0:T(8,128)S(1)}, f32[2,4,16,256]{3,2,1,0:T(8,128)}, u32[]{:S(2)}, u32[]{:S(2)}) collective-permute-start(f32[2,4,16,256]{3,2,1,0:T(8,128)S(1)} %collective-permute-done.1), channel_id=1, source_target_pairs={{0,1},{1,2},{2,3},{3,0},{4,5},{5,6},{6,7},{7,4},{8,9},{9,10},{10,1... | collective-permute-start | bytes 393224 | tf_op jit(solution)/shard_map/ppermute | solution.py:34
  44.2 1.0 %copy-start.2 = (f32[2,32,16,256]{3,2,1,0:T(8,128)}, f32[2,32,16,256]{3,2,1,0:T(8,128)S(1)}, u32[]{:S(2)}) copy-start(f32[2,32,16,256]{3,2,1,0:T(8,128)S(1)} %constant_dynamic-update-slice_fusion) | copy-start | bytes 3145732
  55.4 7.5 %copy-start = (f32[1,256,1024]{2,1,0:T(8,128)S(1)}, f32[1,256,1024]{2,1,0:T(8,128)}, u32[]{:S(2)}) copy-start(f32[1,256,1024]{2,1,0:T(8,128)} %get-tuple-element.10) | copy-start | bytes 3145732
  59.1 22.1 %all-to-all-start.1 = ((f32[8,1,64,512]{3,2,1,0:T(8,128)}), f32[8,1,64,512]{3,2,1,0:T(8,128)S(1)}, u32[]{:S(2)}, u32[]{:S(2)}) async-start(f32[8,1,64,512]{3,2,1,0:T(8,128)} %bitcast.20), calls=%async_computation.1 | async-start | bytes 2097152 | tf_op jit(solution)/shard_map/all_to_all | solution.py:48
